TPU v7x, 256 devices: a whole 4x4x8 slice. The times are simulated.
256 devices in a mesh: tile: 32 (over z_hi, x, core), lev: 4 (over y), sec: 2 (over z_lo).
Axes of the slice: x: 4, y: 4, z: 8 (z_hi: 4, z_lo: 2; z = z_hi * 2 + z_lo), core: 2. Of those that a mesh axis runs over, the one named last changes fastest.
Arguments:
- forcing: float32 [8, 72, 1280, 384], P('sec', 'lev', 'tile'), may hold values from -6 to 6
- courant_x: bfloat16 [72, 1280, 384], P('lev', 'tile'), may hold values from -0.44921875 to 0.44921875
- courant_y: bfloat16 [72, 1280, 384], P('lev', 'tile'), may hold values from -0.44921875 to 0.44921875
- mass_flux: bfloat16 [72, 1280, 384], P('lev', 'tile'), may hold values from 0 to 0.59765625
- limiter_code: int32 [72, 1280, 384], P('lev', 'tile'), may hold values from 0 to 15
- seam_code: int32 [32, 2], replicated, may hold values from 0 to 1
- level_weight: float32 [72], P('lev'), may hold values from 0.02 to 0.5
- sector_share: float32 [8, 1280, 384], P('sec', 'tile'), may hold values from 0.1 to 1
- flux_cell: int32 [1024, 480], P('tile'), may hold values from 0 to 15359
Outputs:
- adjoint_start: float32 [8, 72, 1280, 384], P('sec', 'lev', 'tile')
- flux_sensitivity: float32 [491520], P('tile')
All inputs are finite; a program needn't handle non-finite values.
Results may differ from a plain program's by a relative error of at most 0.0003.
Values sent between devices are 32-bit elements; how exact they have to be, the bound alone decides.
A program may use at most 128 MiB of HBM per device.

v0:
```python
import jax
import jax.numpy as jnp
from jax import lax
from jax.sharding import PartitionSpec as P

FL_DEV = 15360


def from_behind(value, axis, steps):
    count = lax.axis_size(axis)
    initial, last = (max(0, -steps), min(count, count - steps))
    return lax.ppermute(value, axis, [(source, source + steps) for source in range(initial, last)])


def extended_2(value, sides, width):
    for axis, dim in sides:
        devices, length = (lax.axis_size(axis), value.shape[dim])
        up = [(i, (i + 1) % devices) for i in range(devices)]
        down = [(j, i) for i, j in up]
        last = lax.slice_in_dim(value, length - width, length, axis=dim)
        initial = lax.slice_in_dim(value, 0, width, axis=dim)
        before = lax.ppermute(last, axis, up)
        after = lax.ppermute(initial, axis, down)
        value = jnp.concatenate([before, value, after], axis=dim)
    return value


def coefficients(courant, codes, bit):
    value = courant.astype(jnp.float32)
    limited = jnp.bitwise_and(jnp.right_shift(codes, bit), 1).astype(jnp.float32)
    spread = 0.5 * jnp.abs(value) * (1.0 - jnp.abs(value))
    ahead = jnp.maximum(value, 0.0) - limited * spread
    behind = jnp.minimum(value, 0.0) + limited * spread
    return (ahead, behind)


def flipped(rim, flag):
    return jnp.where(flag, rim[..., ::-1], rim)


def vertical(adjoint, mixing, at_top):
    above = from_behind(adjoint[:, :1], "lev", -1)
    above = jnp.where(at_top, adjoint[:, -1:], above)
    upper = jnp.concatenate([adjoint[:, 1:], above], axis=1)
    return adjoint + mixing * (upper - adjoint)


def sweep_second(adjoint, courant, codes, bit):
    ahead, behind = coefficients(courant, codes, bit)
    following = jnp.concatenate([adjoint[..., 1:], adjoint[..., -1:]], axis=-1)
    previous = jnp.concatenate([adjoint[..., :1], adjoint[..., :-1]], axis=-1)
    return adjoint + ahead * (following - adjoint) + behind * (adjoint - previous)


def sweep_first(adjoint, courant, codes, bit, flip_left, flip_right):
    ahead, behind = coefficients(courant, codes, bit)
    extended = extended_2(adjoint, (("tile", 2),), 1)
    left_rim = flipped(extended[:, :, :1], flip_left)
    right_rim = flipped(extended[:, :, -1:], flip_right)
    following = jnp.concatenate([adjoint[:, :, 1:], right_rim], axis=2)
    previous = jnp.concatenate([left_rim, adjoint[:, :, :-1]], axis=2)
    return adjoint + ahead * (following - adjoint) + behind * (adjoint - previous)


def shards(
    forcing,
    courant_x,
    courant_y,
    mass_flux,
    limiter_code,
    seam_code,
    level_weight,
    sector_share,
    flux_cell,
):
    mixing = mass_flux.astype(jnp.float32)
    at_top = lax.axis_index("lev") == lax.axis_size("lev") - 1
    tile_count = lax.axis_size("tile")
    tile_rank = lax.axis_index("tile")
    place = jnp.remainder(tile_rank + tile_count, tile_count)
    seams_here = lax.dynamic_index_in_dim(seam_code, place, 0, keepdims=False) == 1
    adjoint = forcing
    for turn_index in (1, 0):
        adjoint = vertical(adjoint, mixing, at_top)
        adjoint = sweep_second(adjoint, courant_y, limiter_code, 2 * turn_index + 1)
        adjoint = sweep_first(
            adjoint, courant_x, limiter_code, 2 * turn_index, seams_here[0], seams_here[1]
        )
    partial_value = jnp.einsum(
        "sxy,l,slxy->xy", sector_share, level_weight, adjoint, precision=lax.Precision.HIGHEST
    )
    columns = partial_value.reshape(tile_count, -1)
    totals = lax.psum(columns, ("lev", "sec"))
    received = lax.all_to_all(totals, "tile", split_axis=0, concat_axis=0, tiled=True)
    flux_sensitivity = jax.ops.segment_sum(
        received.reshape(-1), flux_cell.reshape(-1), num_segments=FL_DEV
    )
    return (adjoint, flux_sensitivity)


def solution(mesh):
    placed = (
        P("sec", "lev", "tile", None),
        P("lev", "tile", None),
        P("lev", "tile", None),
        P("lev", "tile", None),
        P("lev", "tile", None),
        P(),
        P("lev"),
        P("sec", "tile", None),
        P("tile", None),
    )
    return jax.shard_map(
        shards,
        mesh=mesh,
        in_specs=placed,
        out_specs=(P("sec", "lev", "tile", None), P("tile")),
        check_vma=False,
    )
```

profile of v0, /device:TPU:1, one launch (start us, length us, event | category | flops | bytes accessed | tf_op | source)
XLA Modules:
  0.0 220.0 jit_solution(4765529639356526114)
XLA Ops:
  0.6 0.0 copy-start
  0.6 0.0 slice-start
  0.7 1.1 slice.78
  1.8 0.0 slice-start.1
  1.8 1.4 collective-permute-start
  3.2 5.8 %fusion.28 = (f32[18,40,384]{2,1,0:T(8,128)}, f32[18,40,384]{2,1,0:T(8,128)}, f32[18,40,384]{2,1,0:T(8,128)}, f32[18,40,384]{2,1,0:T(8,128)}, f32[18,40,384]{2,1...) fusion(bf16[18,40,384]{2,1,0:T(8,128)(2,1)} %param.10, ...), kind=kLoop, calls=%fused_computation.45 | loop fusion | flops 10506240 | bytes 11059200 | tf_op jit(solution)/shard_map/sub | solution.py:32
  9.0 0.0 slice-done
  9.0 0.0 copy-start.10
  9.0 2.3 %slice.76 = f32[4,17,40,384]{3,2,1,0:T(8,128)} slice(f32[4,18,40,384]{3,2,1,0:T(8,128)S(1)} %bitcast.18), slice={[0:4], [1:18], [0:40], [0:384]} | slice | bytes 8355840 | tf_op jit(solution)/shard_map/slice | solution.py:44
  11.3 0.1 convert_element_type.23
  11.4 0.1 dynamic-slice_compare_fusion
  11.5 0.5 fusion.48
  12.0 0.0 collective-permute-done
  12.0 1.0 slice_select_fusion.1
  13.0 4.2 %fusion.3 = f32[4,18,40,384]{3,2,1,0:T(8,128)S(1)} fusion(f32[4,18,40,384]{3,2,1,0:T(8,128)} %param.9, f32[4,1,40,384]{3,2,1,0:T(8,128)S(1)} %slice_select_fusion.1, f32[4,17,40,384]{3,2,1,0:T(8,128)} %slice.76, f32[18,40,384]{2,1,0:T(8,128)S(1)} %convert_element_type.23), kind=kLoop, calls=%fused_computation.5 | loop fusion | flops 4423680 | bytes 14376960 | tf_op jit(solution)/shard_map/add | solution.py:45
  17.2 1.6 fusion.46
  18.8 1.4 fusion.47
  20.2 3.7 %fusion.6 = f32[4,18,40,384]{3,2,1,0:T(8,128)S(1)} fusion(f32[4,18,40,384]{3,2,1,0:T(8,128)S(1)} %fusion.3, f32[4,18,40,1]{3,2,1,0:T(8,128)} %get-tuple-element.17, f32[4,18,40,383]{3,2,1,0:T(8,128)S(1)} %get-tuple-element.19, f32[4,18,40,383]{3,2,1,0:T(8,128)S(1)} %get-tuple-element.18, f32[4,18,40,1]{3,2,1,0:T(8,128)S(1)} %get-tuple-element.16, ...), kind=kLoop, calls=%fused_computation.9 | loop fusion | flops 8847360 | bytes 19906560 | tf_op jit(solution)/shard_map/add | solution.py:52
  23.9 0.0 copy-start.2
  23.9 0.2 fusion.44
  24.1 3.3 %collective-permute-start.1 = (f32[4,18,1,384]{3,1,2,0:T(8,128)S(1)}, f32[4,18,1,384]{3,1,2,0:T(8,128)S(1)}, u32[]{:S(2)}, u32[]{:S(2)}) collective-permute-start(f32[4,18,1,384]{3,1,2,0:T(8,128)S(1)} %copy.26), channel_id=1, source_target_pairs={{8,0},{16,8},{24,16},{32,24},{40,32},{48,40},{56,48},{64,56},{72,6... | collective-permute-start | bytes 331784 | tf_op jit(solution)/shard_map/ppermute | solution.py:23
  27.4 0.1 collective-permute-start.2
  27.5 4.1 %fusion.45 = (f32[4,18,39,384]{3,2,1,0:T(8,128)}, f32[4,18,39,384]{3,2,1,0:T(8,128)}) fusion(f32[4,18,40,384]{3,2,1,0:T(8,128)S(1)} %fusion.6), kind=kLoop, calls=%fused_computation.74 | loop fusion | bytes 17252352 | tf_op jit(solution)/shard_map/slice | solution.py:61
  31.6 0.0 collective-permute-done.1
  31.6 0.1 copy.27
  31.7 0.7 rev.12
  32.4 2.2 collective-permute-done.2
  34.6 0.1 copy.30
  34.7 0.7 rev.13
  35.4 0.8 broadcast_select_fusion.3
  36.2 0.8 broadcast_select_fusion.1
  37.0 5.9 %fusion.10 = f32[4,18,40,384]{3,2,1,0:T(8,128)S(1)} fusion(f32[4,18,40,384]{3,2,1,0:T(8,128)} %copy-done.2, f32[4,18,1,384]{3,2,1,0:T(1,128)S(1)} %broadcast_select_fusion.3, f32[4,18,39,384]{3,2,1,0:T(8,128)} %get-tuple-element.15, f32[4,18,39,384]{3,2,1,0:T(8,128)} %get-tuple-element.14, f32[4,18,1,384]{3,2,1,0:T(1,128)S(1)} %broadcast_select_fusion.1, ...), kind=kLoop, calls=%fused_computation.15 | loop fusion | flops 8847360 | bytes 19906560 | tf_op jit(solution)/shard_map/add | solution.py:62
  42.9 1.5 collective-permute-start.3
  44.4 0.3 slice.108
  44.7 5.8 %collective-permute-done.3 = f32[4,1,40,384]{3,2,1,0:T(8,128)S(1)} collective-permute-done((f32[4,1,40,384]{3,2,1,0:T(8,128)S(1)}, f32[4,1,40,384]{3,2,1,0:T(8,128)S(1)}, u32[]{:S(2)}, u32[]{:S(2)}) %collective-permute-start.3) | collective-permute-done | bytes 245792 | tf_op jit(solution)/shard_map/ppermute | solution.py:12
  50.5 0.7 fusion.13
  51.2 0.5 fusion.42
  51.7 1.4 fusion.43
  53.1 3.5 %fusion.16 = f32[4,18,40,384]{3,2,1,0:T(8,128)S(1)} fusion(f32[4,18,40,384]{3,2,1,0:T(8,128)S(1)} %fusion.13, f32[4,18,40,1]{3,2,1,0:T(8,128)S(1)} %get-tuple-element.9, f32[4,18,40,383]{3,2,1,0:T(8,128)S(1)} %get-tuple-element.11, f32[4,18,40,383]{3,2,1,0:T(8,128)S(1)} %get-tuple-element.10, f32[4,18,40,1]{3,2,1,0:T(8,128)S(1)} %get-tuple-element.8, ...), kind=kLoop, calls=%fused_computation.24 | loop fusion | flops 8847360 | bytes 19906560 | tf_op jit(solution)/shard_map/add | solution.py:52
  56.6 0.0 copy-start.1
  56.6 0.2 fusion.40
  56.8 9.9 %collective-permute-start.4 = (f32[4,18,1,384]{3,1,2,0:T(8,128)S(1)}, f32[4,18,1,384]{3,1,2,0:T(8,128)S(1)}, u32[]{:S(2)}, u32[]{:S(2)}) collective-permute-start(f32[4,18,1,384]{3,1,2,0:T(8,128)S(1)} %copy.32), channel_id=1, source_target_pairs={{8,0},{16,8},{24,16},{32,24},{40,32},{48,40},{56,48},{64,56},{72,6... | collective-permute-start | bytes 331784 | tf_op jit(solution)/shard_map/ppermute | solution.py:23
  66.7 0.1 collective-permute-start.5
  66.8 4.1 %fusion.41 = (f32[4,18,39,384]{3,2,1,0:T(8,128)}, f32[4,18,39,384]{3,2,1,0:T(8,128)}) fusion(f32[4,18,40,384]{3,2,1,0:T(8,128)S(1)} %fusion.16), kind=kLoop, calls=%fused_computation.70 | loop fusion | bytes 17252352 | tf_op jit(solution)/shard_map/slice | solution.py:61
  70.9 0.0 collective-permute-done.4
  70.9 0.1 copy.33
  71.0 0.7 rev.14
  71.7 0.0 collective-permute-done.5
  71.7 0.1 copy.36
  71.9 0.7 rev.15
  72.6 0.8 broadcast_select_fusion.2
  73.4 0.8 broadcast_select_fusion
  74.2 5.7 %fusion.20 = f32[4,18,40,384]{3,2,1,0:T(8,128)S(1)} fusion(f32[4,18,40,384]{3,2,1,0:T(8,128)} %copy-done.1, f32[4,18,1,384]{3,2,1,0:T(1,128)S(1)} %broadcast_select_fusion.2, f32[4,18,39,384]{3,2,1,0:T(8,128)} %get-tuple-element.7, f32[4,18,39,384]{3,2,1,0:T(8,128)} %get-tuple-element.6, f32[4,18,1,384]{3,2,1,0:T(1,128)S(1)} %broadcast_select_fusion, ...), kind=kLoop, calls=%fused_computation.30 | loop fusion | flops 8847360 | bytes 19906560 | tf_op jit(solution)/shard_map/add | solution.py:62
  79.9 0.0 copy-start.3
  79.9 2.1 copy-done.3
  82.0 4.4 %fusion = f32[1,4,40,384]{3,0,2,1:T(1,128)S(1)} fusion(f32[4,18,40,384]{3,2,1,0:T(8,128)S(1)} %fusion.20, f32[18]{0:T(128)S(1)} %copy-done), kind=kOutput, calls=%fused_computation.1 | convolution fusion | flops 13271040 | bytes 4669512 | tf_op jit(solution)/shard_map/sxy,l,slxy->xy/dot_general | solution.py:89
  86.4 0.1 all_to_all.6
  86.5 27.3 %psum.7 = f32[32,1,480]{2,1,0:T(1,128)} all-reduce(f32[32,1,480]{2,1,0:T(1,128)S(1)} %all_to_all.6), channel_id=1, replica_groups=mesh['tile'=32,'lev'=4,'sec'=2] {'lev','sec'}, use_global_device_ids=true, to_apply=%region_0.1 | all-reduce | flops 15360 | bytes 122880 | tf_op jit(solution)/shard_map/psum | solution.py:93
  113.9 14.8 %all-to-all-start = ((f32[32,1,480]{2,1,0:T(1,128)}), f32[32,1,480]{2,1,0:T(1,128)S(1)}, u32[]{:S(2)}, u32[]{:S(2)}) async-start(f32[32,1,480]{2,1,0:T(1,128)} %psum.7), calls=%async_computation | async-start | bytes 131072 | tf_op jit(solution)/shard_map/all_to_all | solution.py:94
  128.7 0.1 reshape.33
  128.8 9.9 %all-to-all-done = f32[32,1,480]{2,1,0:T(1,128)S(1)} async-done(((f32[32,1,480]{2,1,0:T(1,128)}), f32[32,1,480]{2,1,0:T(1,128)S(1)}, u32[]{:S(2)}, u32[]{:S(2)}) %all-to-all-start) | async-done | bytes 61472 | tf_op jit(solution)/shard_map/all_to_all | solution.py:94
  138.7 0.2 reduce.1
  138.9 0.1 reshape.35
  139.0 81.0 %scatter_custom_fusion = f32[15360]{0:T(1024)} fusion(s32[15360]{0:T(1024)S(1)} %reshape.33, f32[15360]{0:T(1024)S(1)} %reshape.35, f32[]{:T(128)} %constant.16.clone.1), kind=kCustom, calls=%fused_computation.65 | custom fusion | flops 15360 | bytes 61444 | tf_op jit(solution)/shard_map/scatter-add | solution.py:95
  (25 shorter events, 0.2 us)
Async XLA Ops:
  0.6 81.3 %copy-start = (f32[18]{0:T(128)S(1)}, f32[18]{0:T(128)}, u32[]{:S(2)}) copy-start(f32[18]{0:T(128)} %param.15) | copy-start | bytes 220
  0.6 8.3 %slice-start = ((s8[4423680]{0:T(1024)(128)(4,1)}), s8[4194304]{0:T(1024)(128)(4,1)S(1)}, s32[]{:S(2)}) async-start(s8[4423680]{0:T(1024)(128)(4,1)} %bitcast.17), calls=%async_computation.1 | async-start | bytes 8388608
  1.8 7.2 %slice-start.1 = ((s8[4423680]{0:T(1024)(128)(4,1)}), s8[229376]{0:T(1024)(128)(4,1)S(1)}, s32[]{:S(2)}) async-start(s8[4423680]{0:T(1024)(128)(4,1)} %bitcast.17), calls=%async_computation.2 | async-start | bytes 458752
  1.8 10.2 %collective-permute-start = (f32[4,1,40,384]{3,2,1,0:T(8,128)S(1)}, f32[4,1,40,384]{3,2,1,0:T(8,128)S(1)}, u32[]{:S(2)}, u32[]{:S(2)}) collective-permute-start(f32[4,1,40,384]{3,2,1,0:T(8,128)S(1)} %slice.78), channel_id=1, source_target_pairs={{2,0},{4,2},{6,4},{3,1},{5,3},{7,5},{10,8},{12,10},{14,12},{11,9},... | collective-permute-start | bytes 737288 | tf_op jit(solution)/shard_map/ppermute | solution.py:12
  9.0 2.3 %copy-start.7 = (bf16[18,40,384]{2,1,0:T(8,128)(2,1)S(1)}, bf16[18,40,384]{2,1,0:T(8,128)(2,1)}, u32[]{:S(2)}) copy-start(bf16[18,40,384]{2,1,0:T(8,128)(2,1)} %param.12) | copy-start | bytes 1658884
  9.0 2.4 %copy-start.10 = (s32[32,2]{0,1:T(2,128)S(1)}, s32[32,2]{0,1:T(2,128)}, u32[]{:S(2)}) copy-start(s32[32,2]{0,1:T(2,128)} %param.14) | copy-start | bytes 772
  23.9 7.7 %copy-start.2 = (f32[4,18,40,384]{3,2,1,0:T(8,128)}, f32[4,18,40,384]{3,2,1,0:T(8,128)S(1)}, u32[]{:S(2)}) copy-start(f32[4,18,40,384]{3,2,1,0:T(8,128)S(1)} %fusion.6) | copy-start | bytes 13271044
  24.1 7.5 %collective-permute-start.1 = (f32[4,18,1,384]{3,1,2,0:T(8,128)S(1)}, f32[4,18,1,384]{3,1,2,0:T(8,128)S(1)}, u32[]{:S(2)}, u32[]{:S(2)}) collective-permute-start(f32[4,18,1,384]{3,1,2,0:T(8,128)S(1)} %copy.26), channel_id=1, source_target_pairs={{8,0},{16,8},{24,16},{32,24},{40,32},{48,40},{56,48},{64,56},{72,6... | collective-permute-start | bytes 331784 | tf_op jit(solution)/shard_map/ppermute | solution.py:23
  27.4 9.6 %copy-start.6 = (f32[18,40,384]{2,1,0:T(8,128)S(1)}, f32[18,40,384]{2,1,0:T(8,128)}, u32[]{:S(2)}) copy-start(f32[18,40,384]{2,1,0:T(8,128)} %get-tuple-element.22) | copy-start | bytes 3317764
  27.4 7.1 %collective-permute-start.2 = (f32[4,18,1,384]{3,1,2,0:T(8,128)S(1)}, f32[4,18,1,384]{3,1,2,0:T(8,128)S(1)}, u32[]{:S(2)}, u32[]{:S(2)}) collective-permute-start(f32[4,18,1,384]{3,1,2,0:T(8,128)S(1)} %copy.29), channel_id=1, source_target_pairs={{0,8},{8,16},{16,24},{24,32},{32,40},{40,48},{48,56},{56,64},{64,7... | collective-permute-start | bytes 331784 | tf_op jit(solution)/shard_map/ppermute | solution.py:22
  42.9 7.6 %collective-permute-start.3 = (f32[4,1,40,384]{3,2,1,0:T(8,128)S(1)}, f32[4,1,40,384]{3,2,1,0:T(8,128)S(1)}, u32[]{:S(2)}, u32[]{:S(2)}) collective-permute-start(f32[4,1,40,384]{3,2,1,0:T(8,128)S(1)} %slice.110), channel_id=1, source_target_pairs={{2,0},{4,2},{6,4},{3,1},{5,3},{7,5},{10,8},{12,10},{14,12},{11,9},... | collective-permute-start | bytes 737288 | tf_op jit(solution)/shard_map/ppermute | solution.py:12
  56.6 14.3 %copy-start.1 = (f32[4,18,40,384]{3,2,1,0:T(8,128)}, f32[4,18,40,384]{3,2,1,0:T(8,128)S(1)}, u32[]{:S(2)}) copy-start(f32[4,18,40,384]{3,2,1,0:T(8,128)S(1)} %fusion.16) | copy-start | bytes 13271044
  56.8 14.1 %collective-permute-start.4 = (f32[4,18,1,384]{3,1,2,0:T(8,128)S(1)}, f32[4,18,1,384]{3,1,2,0:T(8,128)S(1)}, u32[]{:S(2)}, u32[]{:S(2)}) collective-permute-start(f32[4,18,1,384]{3,1,2,0:T(8,128)S(1)} %copy.32), channel_id=1, source_target_pairs={{8,0},{16,8},{24,16},{32,24},{40,32},{48,40},{56,48},{64,56},{72,6... | collective-permute-start | bytes 331784 | tf_op jit(solution)/shard_map/ppermute | solution.py:23
  66.7 7.4 %copy-start.4 = (f32[18,40,384]{2,1,0:T(8,128)S(1)}, f32[18,40,384]{2,1,0:T(8,128)}, u32[]{:S(2)}) copy-start(f32[18,40,384]{2,1,0:T(8,128)} %get-tuple-element.20) | copy-start | bytes 3317764
  66.7 7.4 %copy-start.5 = (f32[18,40,384]{2,1,0:T(8,128)S(1)}, f32[18,40,384]{2,1,0:T(8,128)}, u32[]{:S(2)}) copy-start(f32[18,40,384]{2,1,0:T(8,128)} %get-tuple-element.21) | copy-start | bytes 3317764
  66.7 5.0 %collective-permute-start.5 = (f32[4,18,1,384]{3,1,2,0:T(8,128)S(1)}, f32[4,18,1,384]{3,1,2,0:T(8,128)S(1)}, u32[]{:S(2)}, u32[]{:S(2)}) collective-permute-start(f32[4,18,1,384]{3,1,2,0:T(8,128)S(1)} %copy.35), channel_id=1, source_target_pairs={{0,8},{8,16},{16,24},{24,32},{32,40},{40,48},{48,56},{56,64},{64,7... | collective-permute-start | bytes 331784 | tf_op jit(solution)/shard_map/ppermute | solution.py:22
  79.9 2.1 copy-start.3
  82.0 4.4 %copy-start.8 = (f32[4,40,384]{2,1,0:T(8,128)S(1)}, f32[4,40,384]{2,1,0:T(8,128)}, u32[]{:S(2)}) copy-start(f32[4,40,384]{2,1,0:T(8,128)} %param.16) | copy-start | bytes 737284
  82.0 46.7 %copy-start.9 = (s32[32,480]{1,0:T(8,128)S(1)}, s32[32,480]{1,0:T(8,128)}, u32[]{:S(2)}) copy-start(s32[32,480]{1,0:T(8,128)} %param.17) | copy-start | bytes 184324
  113.9 24.8 %all-to-all-start = ((f32[32,1,480]{2,1,0:T(1,128)}), f32[32,1,480]{2,1,0:T(1,128)S(1)}, u32[]{:S(2)}, u32[]{:S(2)}) async-start(f32[32,1,480]{2,1,0:T(1,128)} %psum.7), calls=%async_computation | async-start | bytes 131072 | tf_op jit(solution)/shard_map/all_to_all | solution.py:94
where the time goes:
time: 220 us
  other arithmetic  115 us (52%)
  starting transfers between devices  31.1 us (14%)
  blocking collectives  27.3 us (12%)
  local copies, waits for them, and re-layouts  23.3 us (11%)
  waiting for transfers between devices  17.9 us (8%)
  matrix products  4.36 us (2%)
    scatter-add x1, other arithmetic, shards(): jax.ops.segment_sum(received.reshape(-1), flux_cell.reshape(-1), num_segm...  81 us
    psum x1, blocking collectives, shards(): totals = lax.psum(columns, ('lev', 'sec'))  27.3 us
    all_to_all x1, starting transfers between devices, shards(): lax.all_to_all(totals, 'tile', split_axis=0, concat_axis=0, tiled=True)  14.8 us
    ppermute x2, starting transfers between devices, extended_2(): after = lax.ppermute(initial, axis, down)  13.2 us
    add x2, other arithmetic, sweep_first(): adjoint + ahead * (following - adjoint) + behind * (adjoint - previous)  11.6 us
    all_to_all x1, waiting for transfers between devices, shards(): lax.all_to_all(totals, 'tile', split_axis=0, concat_axis=0, tiled=True)  9.88 us
    slice x2, local copies, waits for them, and re-layouts, sweep_first(): previous = jnp.concatenate([left_rim, adjoint[:, :, :-1]], axis=2)  8.13 us
    add x2, other arithmetic, sweep_second(): adjoint + ahead * (following - adjoint) + behind * (adjoint - previous)  7.2 us
  transfers between devices with their start and end apart: 7, of which 3 were waited for; matrix products, arithmetic and copies ran while one was open for 9% of the time, Pallas kernels for 0%

commit v1 on v0

--- a/solution.py
+++ b/solution.py
@@ -90,7 +90,7 @@
         "sxy,l,slxy->xy", sector_share, level_weight, adjoint, precision=lax.Precision.HIGHEST
     )
     columns = partial_value.reshape(tile_count, -1)
-    totals = lax.psum(columns, ("lev", "sec"))
+    totals = lax.psum(lax.psum(columns, "sec"), "lev")
     received = lax.all_to_all(totals, "tile", split_axis=0, concat_axis=0, tiled=True)
     flux_sensitivity = jax.ops.segment_sum(
         received.reshape(-1), flux_cell.reshape(-1), num_segments=FL_DEV

time: 220 us -> 212 us (0.964)
  blocking collectives: 27.3 us -> 20.6 us
    psum x1 -> x2, blocking collectives: 27.3 us -> 20.6 us  [shards(): totals = lax.psum(lax.psum(columns, 'sec'), 'lev')]
where the time goes in v1:
time: 212 us
  other arithmetic  115 us (54%)
  starting transfers between devices  29.6 us (14%)
  local copies, waits for them, and re-layouts  23.4 us (11%)
  blocking collectives  20.6 us (10%)
  waiting for transfers between devices  18 us (8%)
  matrix products  4.36 us (2%)
    scatter-add x1, other arithmetic, shards(): jax.ops.segment_sum(received.reshape(-1), flux_cell.reshape(-1), num_segm...  81 us
    psum x2, blocking collectives, shards(): totals = lax.psum(lax.psum(columns, 'sec'), 'lev')  20.6 us
    all_to_all x1, starting transfers between devices, shards(): lax.all_to_all(totals, 'tile', split_axis=0, concat_axis=0, tiled=True)  13.3 us
    ppermute x2, starting transfers between devices, extended_2(): after = lax.ppermute(initial, axis, down)  13.2 us
    add x2, other arithmetic, sweep_first(): adjoint + ahead * (following - adjoint) + behind * (adjoint - previous)  11.6 us
    all_to_all x1, waiting for transfers between devices, shards(): lax.all_to_all(totals, 'tile', split_axis=0, concat_axis=0, tiled=True)  9.98 us
    slice x2, local copies, waits for them, and re-layouts, sweep_first(): previous = jnp.concatenate([left_rim, adjoint[:, :, :-1]], axis=2)  8.12 us
    add x2, other arithmetic, sweep_second(): adjoint + ahead * (following - adjoint) + behind * (adjoint - previous)  7.2 us
  transfers between devices with their start and end apart: 7, of which 3 were waited for; matrix products, arithmetic and copies ran while one was open for 9% of the time, Pallas kernels for 0%

profile of v1, /device:TPU:1, one launch (start us, length us, event | category | flops | bytes accessed | tf_op | source)
XLA Modules:
  0.0 212.1 jit_solution(6591119119835102600)
XLA Ops:
  0.6 0.0 copy-start
  0.6 0.0 slice-start
  0.7 1.1 slice.78
  1.8 0.0 slice-start.1
  1.8 1.4 collective-permute-start
  3.2 5.7 %fusion.28 = (f32[18,40,384]{2,1,0:T(8,128)}, f32[18,40,384]{2,1,0:T(8,128)}, f32[18,40,384]{2,1,0:T(8,128)}, f32[18,40,384]{2,1,0:T(8,128)}, f32[18,40,384]{2,1...) fusion(bf16[18,40,384]{2,1,0:T(8,128)(2,1)} %param.10, ...), kind=kLoop, calls=%fused_computation.45 | loop fusion | flops 10506240 | bytes 11059200 | tf_op jit(solution)/shard_map/sub | solution.py:32
  9.0 0.0 copy-start.10
  9.0 2.3 %slice.76 = f32[4,17,40,384]{3,2,1,0:T(8,128)} slice(f32[4,18,40,384]{3,2,1,0:T(8,128)S(1)} %bitcast.18), slice={[0:4], [1:18], [0:40], [0:384]} | slice | bytes 8355840 | tf_op jit(solution)/shard_map/slice | solution.py:44
  11.3 0.1 convert_element_type.23
  11.4 0.1 dynamic-slice_compare_fusion
  11.4 0.6 fusion.48
  12.0 0.0 collective-permute-done
  12.1 1.0 slice_select_fusion.1
  13.0 4.2 %fusion.3 = f32[4,18,40,384]{3,2,1,0:T(8,128)S(1)} fusion(f32[4,18,40,384]{3,2,1,0:T(8,128)} %param.9, f32[4,1,40,384]{3,2,1,0:T(8,128)S(1)} %slice_select_fusion.1, f32[4,17,40,384]{3,2,1,0:T(8,128)} %slice.76, f32[18,40,384]{2,1,0:T(8,128)S(1)} %convert_element_type.23), kind=kLoop, calls=%fused_computation.5 | loop fusion | flops 4423680 | bytes 14376960 | tf_op jit(solution)/shard_map/add | solution.py:45
  17.2 1.6 fusion.46
  18.8 1.4 fusion.47
  20.2 3.7 %fusion.6 = f32[4,18,40,384]{3,2,1,0:T(8,128)S(1)} fusion(f32[4,18,40,384]{3,2,1,0:T(8,128)S(1)} %fusion.3, f32[4,18,40,1]{3,2,1,0:T(8,128)} %get-tuple-element.17, f32[4,18,40,383]{3,2,1,0:T(8,128)S(1)} %get-tuple-element.19, f32[4,18,40,383]{3,2,1,0:T(8,128)S(1)} %get-tuple-element.18, f32[4,18,40,1]{3,2,1,0:T(8,128)S(1)} %get-tuple-element.16, ...), kind=kLoop, calls=%fused_computation.9 | loop fusion | flops 8847360 | bytes 19906560 | tf_op jit(solution)/shard_map/add | solution.py:52
  23.9 0.0 copy-start.2
  23.9 0.2 fusion.44
  24.1 3.3 %collective-permute-start.1 = (f32[4,18,1,384]{3,1,2,0:T(8,128)S(1)}, f32[4,18,1,384]{3,1,2,0:T(8,128)S(1)}, u32[]{:S(2)}, u32[]{:S(2)}) collective-permute-start(f32[4,18,1,384]{3,1,2,0:T(8,128)S(1)} %copy.26), channel_id=1, source_target_pairs={{8,0},{16,8},{24,16},{32,24},{40,32},{48,40},{56,48},{64,56},{72,6... | collective-permute-start | bytes 331784 | tf_op jit(solution)/shard_map/ppermute | solution.py:23
  27.5 0.1 collective-permute-start.2
  27.6 4.1 %fusion.45 = (f32[4,18,39,384]{3,2,1,0:T(8,128)}, f32[4,18,39,384]{3,2,1,0:T(8,128)}) fusion(f32[4,18,40,384]{3,2,1,0:T(8,128)S(1)} %fusion.6), kind=kLoop, calls=%fused_computation.74 | loop fusion | bytes 17252352 | tf_op jit(solution)/shard_map/slice | solution.py:61
  31.6 0.0 collective-permute-done.1
  31.6 0.1 copy.27
  31.8 0.7 rev.12
  32.5 2.2 %collective-permute-done.2 = f32[4,18,1,384]{3,1,2,0:T(8,128)S(1)} collective-permute-done((f32[4,18,1,384]{3,1,2,0:T(8,128)S(1)}, f32[4,18,1,384]{3,1,2,0:T(8,128)S(1)}, u32[]{:S(2)}, u32[]{:S(2)}) %collective-permute-start.2) | collective-permute-done | bytes 110624 | tf_op jit(solution)/shard_map/ppermute | solution.py:22
  34.6 0.1 copy.30
  34.7 0.7 rev.13
  35.4 0.8 broadcast_select_fusion.3
  36.3 0.8 broadcast_select_fusion.1
  37.1 5.9 %fusion.10 = f32[4,18,40,384]{3,2,1,0:T(8,128)S(1)} fusion(f32[4,18,40,384]{3,2,1,0:T(8,128)} %copy-done.2, f32[4,18,1,384]{3,2,1,0:T(1,128)S(1)} %broadcast_select_fusion.3, f32[4,18,39,384]{3,2,1,0:T(8,128)} %get-tuple-element.15, f32[4,18,39,384]{3,2,1,0:T(8,128)} %get-tuple-element.14, f32[4,18,1,384]{3,2,1,0:T(1,128)S(1)} %broadcast_select_fusion.1, ...), kind=kLoop, calls=%fused_computation.15 | loop fusion | flops 8847360 | bytes 19906560 | tf_op jit(solution)/shard_map/add | solution.py:62
  43.1 1.5 collective-permute-start.3
  44.5 0.3 slice.108
  44.8 5.8 %collective-permute-done.3 = f32[4,1,40,384]{3,2,1,0:T(8,128)S(1)} collective-permute-done((f32[4,1,40,384]{3,2,1,0:T(8,128)S(1)}, f32[4,1,40,384]{3,2,1,0:T(8,128)S(1)}, u32[]{:S(2)}, u32[]{:S(2)}) %collective-permute-start.3) | collective-permute-done | bytes 245792 | tf_op jit(solution)/shard_map/ppermute | solution.py:12
  50.7 0.7 fusion.13
  51.4 0.5 fusion.42
  51.8 1.4 fusion.43
  53.2 3.5 %fusion.16 = f32[4,18,40,384]{3,2,1,0:T(8,128)S(1)} fusion(f32[4,18,40,384]{3,2,1,0:T(8,128)S(1)} %fusion.13, f32[4,18,40,1]{3,2,1,0:T(8,128)S(1)} %get-tuple-element.9, f32[4,18,40,383]{3,2,1,0:T(8,128)S(1)} %get-tuple-element.11, f32[4,18,40,383]{3,2,1,0:T(8,128)S(1)} %get-tuple-element.10, f32[4,18,40,1]{3,2,1,0:T(8,128)S(1)} %get-tuple-element.8, ...), kind=kLoop, calls=%fused_computation.24 | loop fusion | flops 8847360 | bytes 19906560 | tf_op jit(solution)/shard_map/add | solution.py:52
  56.7 0.0 copy-start.1
  56.8 0.2 fusion.40
  56.9 9.9 %collective-permute-start.4 = (f32[4,18,1,384]{3,1,2,0:T(8,128)S(1)}, f32[4,18,1,384]{3,1,2,0:T(8,128)S(1)}, u32[]{:S(2)}, u32[]{:S(2)}) collective-permute-start(f32[4,18,1,384]{3,1,2,0:T(8,128)S(1)} %copy.32), channel_id=1, source_target_pairs={{8,0},{16,8},{24,16},{32,24},{40,32},{48,40},{56,48},{64,56},{72,6... | collective-permute-start | bytes 331784 | tf_op jit(solution)/shard_map/ppermute | solution.py:23
  66.9 0.1 collective-permute-start.5
  67.0 4.1 %fusion.41 = (f32[4,18,39,384]{3,2,1,0:T(8,128)}, f32[4,18,39,384]{3,2,1,0:T(8,128)}) fusion(f32[4,18,40,384]{3,2,1,0:T(8,128)S(1)} %fusion.16), kind=kLoop, calls=%fused_computation.70 | loop fusion | bytes 17252352 | tf_op jit(solution)/shard_map/slice | solution.py:61
  71.0 0.0 collective-permute-done.4
  71.0 0.1 copy.33
  71.2 0.7 rev.14
  71.9 0.0 collective-permute-done.5
  71.9 0.1 copy.36
  72.0 0.7 rev.15
  72.7 0.8 broadcast_select_fusion.2
  73.6 0.8 broadcast_select_fusion
  74.4 5.7 %fusion.20 = f32[4,18,40,384]{3,2,1,0:T(8,128)S(1)} fusion(f32[4,18,40,384]{3,2,1,0:T(8,128)} %copy-done.1, f32[4,18,1,384]{3,2,1,0:T(1,128)S(1)} %broadcast_select_fusion.2, f32[4,18,39,384]{3,2,1,0:T(8,128)} %get-tuple-element.7, f32[4,18,39,384]{3,2,1,0:T(8,128)} %get-tuple-element.6, f32[4,18,1,384]{3,2,1,0:T(1,128)S(1)} %broadcast_select_fusion, ...), kind=kLoop, calls=%fused_computation.30 | loop fusion | flops 8847360 | bytes 19906560 | tf_op jit(solution)/shard_map/add | solution.py:62
  80.1 0.0 copy-start.3
  80.1 2.1 copy-done.3
  82.2 4.4 %fusion = f32[1,4,40,384]{3,0,2,1:T(1,128)S(1)} fusion(f32[4,18,40,384]{3,2,1,0:T(8,128)S(1)} %fusion.20, f32[18]{0:T(128)S(1)} %copy-done), kind=kOutput, calls=%fused_computation.1 | convolution fusion | flops 13271040 | bytes 4669512 | tf_op jit(solution)/shard_map/sxy,l,slxy->xy/dot_general | solution.py:89
  86.6 0.1 reshape.28
  86.7 6.9 %psum.14 = f32[32,480]{1,0:T(8,128)S(1)} all-reduce(f32[32,480]{1,0:T(8,128)S(1)} %reshape.28), channel_id=1, replica_groups=mesh['tile'=32,'lev'=4,'sec'=2] {'sec'}, use_global_device_ids=true, to_apply=%region_0.1 | all-reduce | flops 15360 | bytes 122880 | tf_op jit(solution)/shard_map/psum | solution.py:93
  93.6 13.7 %psum.15 = f32[32,1,480]{2,1,0:T(1,128)} all-reduce(f32[32,1,480]{2,1,0:T(1,128)S(1)} %all_to_all.6), channel_id=1, replica_groups=mesh['tile'=32,'lev'=4,'sec'=2] {'lev'}, use_global_device_ids=true, to_apply=%region_1.2 | all-reduce | flops 15360 | bytes 122880 | tf_op jit(solution)/shard_map/psum | solution.py:93
  107.4 13.3 %all-to-all-start = ((f32[32,1,480]{2,1,0:T(1,128)}), f32[32,1,480]{2,1,0:T(1,128)S(1)}, u32[]{:S(2)}, u32[]{:S(2)}) async-start(f32[32,1,480]{2,1,0:T(1,128)} %psum.15), calls=%async_computation | async-start | bytes 131072 | tf_op jit(solution)/shard_map/all_to_all | solution.py:94
  120.7 0.1 reshape.32
  120.8 10.0 %all-to-all-done = f32[32,1,480]{2,1,0:T(1,128)S(1)} async-done(((f32[32,1,480]{2,1,0:T(1,128)}), f32[32,1,480]{2,1,0:T(1,128)S(1)}, u32[]{:S(2)}, u32[]{:S(2)}) %all-to-all-start) | async-done | bytes 61472 | tf_op jit(solution)/shard_map/all_to_all | solution.py:94
  130.8 0.2 reduce.1
  130.9 0.1 reshape.34
  131.0 81.0 %scatter_custom_fusion = f32[15360]{0:T(1024)} fusion(s32[15360]{0:T(1024)S(1)} %reshape.32, f32[15360]{0:T(1024)S(1)} %reshape.34, f32[]{:T(128)} %constant.16.clone.1), kind=kCustom, calls=%fused_computation.65 | custom fusion | flops 15360 | bytes 61444 | tf_op jit(solution)/shard_map/scatter-add | solution.py:95
  (27 shorter events, 0.2 us)
Async XLA Ops:
  0.6 81.5 %copy-start = (f32[18]{0:T(128)S(1)}, f32[18]{0:T(128)}, u32[]{:S(2)}) copy-start(f32[18]{0:T(128)} %param.15) | copy-start | bytes 220
  0.6 8.3 %slice-start = ((s8[4423680]{0:T(1024)(128)(4,1)}), s8[4194304]{0:T(1024)(128)(4,1)S(1)}, s32[]{:S(2)}) async-start(s8[4423680]{0:T(1024)(128)(4,1)} %bitcast.17), calls=%async_computation.1 | async-start | bytes 8388608
  1.8 7.2 %slice-start.1 = ((s8[4423680]{0:T(1024)(128)(4,1)}), s8[229376]{0:T(1024)(128)(4,1)S(1)}, s32[]{:S(2)}) async-start(s8[4423680]{0:T(1024)(128)(4,1)} %bitcast.17), calls=%async_computation.2 | async-start | bytes 458752
  1.8 10.3 %collective-permute-start = (f32[4,1,40,384]{3,2,1,0:T(8,128)S(1)}, f32[4,1,40,384]{3,2,1,0:T(8,128)S(1)}, u32[]{:S(2)}, u32[]{:S(2)}) collective-permute-start(f32[4,1,40,384]{3,2,1,0:T(8,128)S(1)} %slice.78), channel_id=1, source_target_pairs={{2,0},{4,2},{6,4},{3,1},{5,3},{7,5},{10,8},{12,10},{14,12},{11,9},... | collective-permute-start | bytes 737288 | tf_op jit(solution)/shard_map/ppermute | solution.py:12
  9.0 2.3 %copy-start.7 = (bf16[18,40,384]{2,1,0:T(8,128)(2,1)S(1)}, bf16[18,40,384]{2,1,0:T(8,128)(2,1)}, u32[]{:S(2)}) copy-start(bf16[18,40,384]{2,1,0:T(8,128)(2,1)} %param.12) | copy-start | bytes 1658884
  9.0 2.4 %copy-start.10 = (s32[32,2]{0,1:T(2,128)S(1)}, s32[32,2]{0,1:T(2,128)}, u32[]{:S(2)}) copy-start(s32[32,2]{0,1:T(2,128)} %param.14) | copy-start | bytes 772
  23.9 7.7 %copy-start.2 = (f32[4,18,40,384]{3,2,1,0:T(8,128)}, f32[4,18,40,384]{3,2,1,0:T(8,128)S(1)}, u32[]{:S(2)}) copy-start(f32[4,18,40,384]{3,2,1,0:T(8,128)S(1)} %fusion.6) | copy-start | bytes 13271044
  24.1 7.5 %collective-permute-start.1 = (f32[4,18,1,384]{3,1,2,0:T(8,128)S(1)}, f32[4,18,1,384]{3,1,2,0:T(8,128)S(1)}, u32[]{:S(2)}, u32[]{:S(2)}) collective-permute-start(f32[4,18,1,384]{3,1,2,0:T(8,128)S(1)} %copy.26), channel_id=1, source_target_pairs={{8,0},{16,8},{24,16},{32,24},{40,32},{48,40},{56,48},{64,56},{72,6... | collective-permute-start | bytes 331784 | tf_op jit(solution)/shard_map/ppermute | solution.py:23
  27.5 9.6 %copy-start.6 = (f32[18,40,384]{2,1,0:T(8,128)S(1)}, f32[18,40,384]{2,1,0:T(8,128)}, u32[]{:S(2)}) copy-start(f32[18,40,384]{2,1,0:T(8,128)} %get-tuple-element.22) | copy-start | bytes 3317764
  27.5 7.1 %collective-permute-start.2 = (f32[4,18,1,384]{3,1,2,0:T(8,128)S(1)}, f32[4,18,1,384]{3,1,2,0:T(8,128)S(1)}, u32[]{:S(2)}, u32[]{:S(2)}) collective-permute-start(f32[4,18,1,384]{3,1,2,0:T(8,128)S(1)} %copy.29), channel_id=1, source_target_pairs={{0,8},{8,16},{16,24},{24,32},{32,40},{40,48},{48,56},{56,64},{64,7... | collective-permute-start | bytes 331784 | tf_op jit(solution)/shard_map/ppermute | solution.py:22
  43.1 7.6 %collective-permute-start.3 = (f32[4,1,40,384]{3,2,1,0:T(8,128)S(1)}, f32[4,1,40,384]{3,2,1,0:T(8,128)S(1)}, u32[]{:S(2)}, u32[]{:S(2)}) collective-permute-start(f32[4,1,40,384]{3,2,1,0:T(8,128)S(1)} %slice.110), channel_id=1, source_target_pairs={{2,0},{4,2},{6,4},{3,1},{5,3},{7,5},{10,8},{12,10},{14,12},{11,9},... | collective-permute-start | bytes 737288 | tf_op jit(solution)/shard_map/ppermute | solution.py:12
  56.7 14.3 %copy-start.1 = (f32[4,18,40,384]{3,2,1,0:T(8,128)}, f32[4,18,40,384]{3,2,1,0:T(8,128)S(1)}, u32[]{:S(2)}) copy-start(f32[4,18,40,384]{3,2,1,0:T(8,128)S(1)} %fusion.16) | copy-start | bytes 13271044
  56.9 14.1 %collective-permute-start.4 = (f32[4,18,1,384]{3,1,2,0:T(8,128)S(1)}, f32[4,18,1,384]{3,1,2,0:T(8,128)S(1)}, u32[]{:S(2)}, u32[]{:S(2)}) collective-permute-start(f32[4,18,1,384]{3,1,2,0:T(8,128)S(1)} %copy.32), channel_id=1, source_target_pairs={{8,0},{16,8},{24,16},{32,24},{40,32},{48,40},{56,48},{64,56},{72,6... | collective-permute-start | bytes 331784 | tf_op jit(solution)/shard_map/ppermute | solution.py:23
  66.9 7.5 %copy-start.4 = (f32[18,40,384]{2,1,0:T(8,128)S(1)}, f32[18,40,384]{2,1,0:T(8,128)}, u32[]{:S(2)}) copy-start(f32[18,40,384]{2,1,0:T(8,128)} %get-tuple-element.20) | copy-start | bytes 3317764
  66.9 7.5 %copy-start.5 = (f32[18,40,384]{2,1,0:T(8,128)S(1)}, f32[18,40,384]{2,1,0:T(8,128)}, u32[]{:S(2)}) copy-start(f32[18,40,384]{2,1,0:T(8,128)} %get-tuple-element.21) | copy-start | bytes 3317764
  66.9 5.0 %collective-permute-start.5 = (f32[4,18,1,384]{3,1,2,0:T(8,128)S(1)}, f32[4,18,1,384]{3,1,2,0:T(8,128)S(1)}, u32[]{:S(2)}, u32[]{:S(2)}) collective-permute-start(f32[4,18,1,384]{3,1,2,0:T(8,128)S(1)} %copy.35), channel_id=1, source_target_pairs={{0,8},{8,16},{16,24},{24,32},{32,40},{40,48},{48,56},{56,64},{64,7... | collective-permute-start | bytes 331784 | tf_op jit(solution)/shard_map/ppermute | solution.py:22
  80.1 2.1 copy-start.3
  82.2 4.4 %copy-start.8 = (f32[4,40,384]{2,1,0:T(8,128)S(1)}, f32[4,40,384]{2,1,0:T(8,128)}, u32[]{:S(2)}) copy-start(f32[4,40,384]{2,1,0:T(8,128)} %param.16) | copy-start | bytes 737284
  82.2 38.5 %copy-start.9 = (s32[32,480]{1,0:T(8,128)S(1)}, s32[32,480]{1,0:T(8,128)}, u32[]{:S(2)}) copy-start(s32[32,480]{1,0:T(8,128)} %param.17) | copy-start | bytes 184324
  107.4 23.4 %all-to-all-start = ((f32[32,1,480]{2,1,0:T(1,128)}), f32[32,1,480]{2,1,0:T(1,128)S(1)}, u32[]{:S(2)}, u32[]{:S(2)}) async-start(f32[32,1,480]{2,1,0:T(1,128)} %psum.15), calls=%async_computation | async-start | bytes 131072 | tf_op jit(solution)/shard_map/all_to_all | solution.py:94
